TPU v7x, 128 devices: a whole 4x4x4 slice. The times are simulated.
128 devices in a mesh: dp: 16 (over x, y), expert: 8 (over z, core).
Axes of the slice: x: 4, y: 4, z: 4, core: 2. Of those that a mesh axis runs over, the one named last changes fastest.
Arguments:
- context: bfloat16 [8192, 4096], P('dp'), may hold values from -6 to 6
- out_weight: bfloat16 [4096, 4096], P('dp', 'expert'), may hold values from -0.09375 to 0.09375
- residual: bfloat16 [8192, 4096], P('dp', 'expert'), may hold values from -6 to 6
- gate_weight: bfloat16 [8, 4096, 8192], P('expert', None, 'dp'), may hold values from -0.09375 to 0.09375
- up_weight: bfloat16 [8, 4096, 8192], P('expert', None, 'dp'), may hold values from -0.09375 to 0.09375
- down_weight: bfloat16 [8, 8192, 4096], P('expert', 'dp'), may hold values from -0.0625 to 0.0625
- gate_values: float32 [8, 512], P('expert'), may hold values from 0.2 to 1
- chosen_blocks: int32 [8, 4], replicated, may hold values from 0 to 63, as said below
- block_counts: int32 [8], replicated, may hold values from 1 to 4, as said below
Outputs:
- mixed: bfloat16 [8192, 4096], P('dp', 'expert')
Inputs may be any that keep to these rules, and one draw needn't show every extreme that they name: `chosen_blocks`: within one expert the 4 block numbers are distinct; slots from block_counts on are unused but hold valid block numbers. `block_counts`: some expert uses all 4 slots.
All inputs are finite; a program needn't handle non-finite values.
Results may differ from a plain program's by a relative error of at most 0.008.
Values may be sent and summed in bfloat16 or wider, within the bound.
A program may use at most 128 MiB of HBM per device.

v0:
```python
import jax
import jax.numpy as jnp
from jax import lax
from jax.sharding import PartitionSpec as P

BLK = 128
CAP = 4


def body(
    context,
    out_weight,
    residual,
    gate_weight,
    up_weight,
    down_weight,
    gate_values,
    chosen_blocks,
    block_counts,
):
    n_dp = lax.axis_size("dp")
    n_expert = lax.axis_size("expert")
    local_tokens = context.shape[0]
    local_width = residual.shape[1]
    model_width = context.shape[1]
    local_blocks = local_tokens // BLK
    n_blocks = local_blocks * n_dp
    piece = BLK // n_dp
    my_expert = lax.axis_index("expert")
    projected = jnp.dot(
        context,
        lax.all_gather(out_weight, "dp", axis=0, tiled=True),
        preferred_element_type=jnp.float32,
    )
    attended = (residual.astype(jnp.float32) + projected).astype(jnp.bfloat16)
    split = attended.reshape(local_blocks, n_dp, piece, local_width).transpose(1, 0, 2, 3)
    pieces = lax.all_to_all(split, "dp", 0, 0, tiled=True)
    pieces = pieces.reshape(n_blocks, piece, local_width)
    slots = jnp.take(pieces, chosen_blocks.reshape(-1), axis=0)
    slots = slots.reshape(n_expert, CAP, piece, local_width)
    mine = lax.all_to_all(slots, "expert", 0, 3, tiled=True)
    mine = mine.reshape(CAP * piece, model_width)
    picked = lax.all_gather(mine, "dp", axis=0, tiled=True)
    w_gate = gate_weight[0]
    w_up = up_weight[0]
    w_down = down_weight[0]
    gate_row = gate_values[0]
    my_count = lax.dynamic_index_in_dim(block_counts, my_expert, 0, keepdims=False)
    live = jnp.arange(CAP * BLK) // BLK < my_count
    scale = jnp.where(live, gate_row, jnp.zeros_like(gate_row))
    scale = scale.reshape(CAP, n_dp, piece).transpose(1, 0, 2).reshape(-1)
    gate = jnp.dot(picked, w_gate, preferred_element_type=jnp.float32)
    upper = jnp.dot(picked, w_up, preferred_element_type=jnp.float32)
    hidden = (jax.nn.silu(gate) * upper).astype(jnp.bfloat16)
    part = jnp.dot(hidden, w_down, preferred_element_type=jnp.float32)
    part = (part * scale[:, None]).astype(jnp.bfloat16)
    summed = lax.psum_scatter(
        part.reshape(n_dp, CAP * piece, model_width), "dp", scatter_dimension=0, tiled=True
    )
    summed = summed.reshape(CAP * piece, n_expert, local_width).transpose(1, 0, 2)
    outs = lax.all_to_all(summed, "expert", 0, 0, tiled=True)
    outs = outs.reshape(n_expert * CAP, piece * local_width)
    selector = chosen_blocks.reshape(-1)[None, :] == jnp.arange(n_blocks)[:, None]
    added = jnp.dot(selector.astype(jnp.bfloat16), outs, preferred_element_type=jnp.float32)
    added = added.reshape(n_dp, local_blocks, piece, local_width)
    back = lax.all_to_all(added, "dp", 0, 0, tiled=True)
    back = back.transpose(1, 0, 2, 3).reshape(local_tokens, local_width)
    total = attended.astype(jnp.float32) + back
    return total.astype(jnp.bfloat16)


def solution(mesh):
    in_specs = (
        P("dp", None),
        P("dp", "expert"),
        P("dp", "expert"),
        P("expert", None, "dp"),
        P("expert", None, "dp"),
        P("expert", "dp", None),
        P("expert", None),
        P(),
        P(),
    )
    out_specs = P("dp", "expert")
    return jax.shard_map(body, mesh=mesh, in_specs=in_specs, out_specs=out_specs, check_vma=False)
```

profile of v0, /device:TPU:0, one launch (start us, length us, event | category | flops | bytes accessed | tf_op | source)
XLA Modules:
  0.0 281.9 jit_solution(4458407969886781237)
XLA Ops:
  6.5 0.0 all-gather.3.cloned.1.call-start
  6.5 0.7 all-gather.3.cloned.1.call-update
  7.3 0.8 copy.29
  8.0 0.1 reshape.95
  8.1 0.0 copy-start
  8.1 55.3 %all-gather.3.cloned.1.call-done = bf16[4096,512]{1,0:T(8,128)(2,1)} async-done(((bf16[256,512]{1,0:T(8,128)(2,1)}), bf16[4096,512]{1,0:T(8,128)(2,1)}) %all-gather.3.cloned.1.call-update) | async-done | bytes 4194320 | tf_op jit(solution)/shard_map/all_gather | solution.py:32
  63.4 5.8 %fusion.8 = bf16[512,512]{1,0:T(8,128)(2,1)S(1)} fusion(bf16[512,4096]{1,0:T(8,128)(2,1)} %param.9, bf16[4096,512]{1,0:T(8,128)(2,1)} %all-gather.3.cloned.1.call-done, bf16[512,512]{1,0:T(8,128)(2,1)} %param.11), kind=kOutput, calls=%fused_computation.9 | convolution fusion | flops 2148270080 | bytes 9437184 | tf_op jit(solution)/shard_map/dot_general | solution.py:30
  69.2 0.0 copy-start.1
  69.3 0.0 copy-start.5
  69.3 0.8 copy.49
  70.1 5.3 %all-to-all-start = ((bf16[16,4,8,512]{3,2,1,0:T(8,128)(2,1)}), bf16[16,4,8,512]{3,2,1,0:T(8,128)(2,1)S(1)}, u32[]{:S(2)}, u32[]{:S(2)}) async-start(bf16[16,4,8,512]{3,2,1,0:T(8,128)(2,1)} %bitcast.60), calls=%async_computation | async-start | bytes 1048576 | tf_op jit(solution)/shard_map/all_to_all | solution.py:37
  75.4 0.0 all-gather.5.cloned.1.call-start
  75.4 0.0 copy-done
  75.5 0.1 copy.30
  75.6 11.3 %all-to-all-done = bf16[16,4,8,512]{3,2,1,0:T(8,128)(2,1)S(1)} async-done(((bf16[16,4,8,512]{3,2,1,0:T(8,128)(2,1)}), bf16[16,4,8,512]{3,2,1,0:T(8,128)(2,1)S(1)}, u32[]{:S(2)}, u32[]{:S(2)}) %all-to-all-start) | async-done | bytes 524320 | tf_op jit(solution)/shard_map/all_to_all | solution.py:37
  86.9 0.6 gather_fusion
  87.4 0.1 broadcast_select_fusion
  87.6 11.8 %all_to_all.30 = bf16[8,4,8,512]{3,2,1,0:T(8,128)(2,1)S(1)} all-to-all(bf16[8,4,8,512]{3,2,1,0:T(8,128)(2,1)S(1)} %broadcast_select_fusion), channel_id=1, replica_groups=mesh['dp'=16,'expert'=8] {'expert'}, dimensions={0} | all-to-all | bytes 524288 | tf_op jit(solution)/shard_map/all_to_all | solution.py:41
  99.3 0.1 copy.50
  99.5 0.8 copy.41
  100.3 0.0 all-gather.5.cloned.1.call-update
  100.3 0.0 reduce-scatter.4.cloned.1.call-start
  100.3 0.6 broadcast.96
  100.9 0.0 copy-done.1
  100.9 0.7 reduce.3
  101.6 0.1 squeeze.20
  101.7 0.0 copy-done.5
  101.7 0.7 dynamic_slice.4
  102.4 0.7 select_bitcast_fusion
  103.1 0.1 mul.19
  103.2 44.6 %all-gather.5.cloned.1.call-done = bf16[512,4096]{1,0:T(8,128)(2,1)} async-done(((bf16[32,4096]{1,0:T(8,128)(2,1)}), bf16[512,4096]{1,0:T(8,128)(2,1)}) %all-gather.5.cloned.1.call-update) | async-done | bytes 4194320 | tf_op jit(solution)/shard_map/all_gather | solution.py:43
  147.8 0.0 copy-start.2
  147.8 0.0 copy-start.4
  147.8 5.9 %fusion.3 = f32[512,512]{1,0:T(8,128)S(1)} fusion(bf16[512,4096]{1,0:T(8,128)(2,1)} %all-gather.5.cloned.1.call-done, bf16[1,4096,512]{2,1,0:T(8,128)(2,1)} %param.12), kind=kOutput, calls=%fused_computation.5 | convolution fusion | flops 2147483648 | bytes 9437184 | tf_op jit(solution)/shard_map/dot_general | solution.py:52
  153.7 0.0 copy-done.2
  153.7 0.0 copy-done.4
  153.8 0.0 copy-start.3
  153.8 2.4 fusion.9
  156.2 0.0 copy-done.3
  156.2 4.3 %multiply_convert_fusion = bf16[512,4096]{1,0:T(8,128)(2,1)} fusion(bf16[512,512]{1,0:T(8,128)(2,1)S(1)} %fusion.9, bf16[1,512,4096]{2,1,0:T(8,128)(2,1)S(1)} %copy-done.3, f32[512]{0:T(512)S(1)} %mul.19), kind=kOutput, calls=%fused_computation.1 | convolution fusion | flops 2151677952 | bytes 8914944 | tf_op jit(solution)/shard_map/dot_general | solution.py:55
  160.5 0.0 reduce-scatter.4.cloned.1.call-update
  160.6 77.4 %reduce-scatter.4.cloned.1.call-done = bf16[1,32,4096]{2,1,0:T(8,128)(2,1)} async-done(((bf16[16,32,4096]{2,1,0:T(8,128)(2,1)}), bf16[1,32,4096]{2,1,0:T(8,128)(2,1)}) %reduce-scatter.4.cloned.1.call-update) | async-done | bytes 262160
  237.9 1.0 copy.42
  239.0 0.8 copy.35
  239.7 4.4 %all-to-all-start.2 = ((bf16[8,32,512]{2,1,0:T(8,128)(2,1)}), bf16[8,32,512]{2,1,0:T(8,128)(2,1)S(1)}, u32[]{:S(2)}, u32[]{:S(2)}) async-start(bf16[8,32,512]{2,1,0:T(8,128)(2,1)} %copy.35), calls=%async_computation.2 | async-start | bytes 524288 | tf_op jit(solution)/shard_map/all_to_all | solution.py:61
  244.1 0.1 eq.26
  244.2 7.5 %all-to-all-done.2 = bf16[8,32,512]{2,1,0:T(8,128)(2,1)S(1)} async-done(((bf16[8,32,512]{2,1,0:T(8,128)(2,1)}), bf16[8,32,512]{2,1,0:T(8,128)(2,1)S(1)}, u32[]{:S(2)}, u32[]{:S(2)}) %all-to-all-start.2) | async-done | bytes 262176 | tf_op jit(solution)/shard_map/all_to_all | solution.py:61
  251.7 0.1 reshape.99
  251.8 0.3 fusion.13
  252.1 0.6 copy.37
  252.8 21.5 %all_to_all.31 = f32[16,4,8,512]{3,2,1,0:T(8,128)S(1)} all-to-all(f32[16,4,8,512]{3,2,1,0:T(8,128)S(1)} %copy.37), channel_id=1, replica_groups=mesh['dp'=16,'expert'=8] {'dp'}, dimensions={0} | all-to-all | bytes 2097152 | tf_op jit(solution)/shard_map/all_to_all | solution.py:66
  274.3 0.1 copy.38
  274.3 1.0 fusion.12
  (5 shorter events, 0.0 us)
Async XLA Ops:
  6.5 56.9 %all-gather.3.cloned.1.call-start = ((), (), s32[]{:S(2)}) async-start(), calls=%async_computation.5 | async-start | bytes 4456448 | tf_op jit(solution)/shard_map/all_gather | solution.py:32
  8.1 67.3 %copy-start = (s32[8,4]{0,1:T(4,128)S(1)}, s32[8,4]{0,1:T(4,128)}, u32[]{:S(2)}) copy-start(s32[8,4]{0,1:T(4,128)} %param.16) | copy-start | bytes 388
  69.2 31.7 %copy-start.1 = (f32[1,512]{1,0:T(1,128)S(1)}, f32[1,512]{1,0:T(1,128)}, u32[]{:S(2)}) copy-start(f32[1,512]{1,0:T(1,128)} %param.15) | copy-start | bytes 6148
  69.3 32.4 %copy-start.5 = (s32[8]{0:T(128)S(1)}, s32[8]{0:T(128)}, u32[]{:S(2)}) copy-start(s32[8]{0:T(128)} %param.17) | copy-start | bytes 100
  70.1 16.8 %all-to-all-start = ((bf16[16,4,8,512]{3,2,1,0:T(8,128)(2,1)}), bf16[16,4,8,512]{3,2,1,0:T(8,128)(2,1)S(1)}, u32[]{:S(2)}, u32[]{:S(2)}) async-start(bf16[16,4,8,512]{3,2,1,0:T(8,128)(2,1)} %bitcast.60), calls=%async_computation | async-start | bytes 1048576 | tf_op jit(solution)/shard_map/all_to_all | solution.py:37
  75.4 72.4 %all-gather.5.cloned.1.call-start = ((), (), s32[]{:S(2)}) async-start(), calls=%async_computation.6 | async-start | bytes 4456448 | tf_op jit(solution)/shard_map/all_gather | solution.py:43
  100.3 137.6 %reduce-scatter.4.cloned.1.call-start = ((), (), s32[]{:S(2)}) async-start(), calls=%async_computation.7 | async-start | bytes 4456448
  147.8 5.9 %copy-start.2 = (bf16[1,4096,512]{2,1,0:T(8,128)(2,1)S(1)}, bf16[1,4096,512]{2,1,0:T(8,128)(2,1)}, u32[]{:S(2)}) copy-start(bf16[1,4096,512]{2,1,0:T(8,128)(2,1)} %param.13) | copy-start | bytes 12582916
  147.8 5.9 %copy-start.4 = (bf16[512,4096]{1,0:T(8,128)(2,1)S(1)}, bf16[512,4096]{1,0:T(8,128)(2,1)}, u32[]{:S(2)}) copy-start(bf16[512,4096]{1,0:T(8,128)(2,1)} %all-gather.5.cloned.1.call-done) | copy-start | bytes 12582916
  153.8 2.5 copy-start.3
  239.7 11.9 %all-to-all-start.2 = ((bf16[8,32,512]{2,1,0:T(8,128)(2,1)}), bf16[8,32,512]{2,1,0:T(8,128)(2,1)S(1)}, u32[]{:S(2)}, u32[]{:S(2)}) async-start(bf16[8,32,512]{2,1,0:T(8,128)(2,1)} %copy.35), calls=%async_computation.2 | async-start | bytes 524288 | tf_op jit(solution)/shard_map/all_to_all | solution.py:61
Sparse Core Ops, SparseCore 0:
  9.5 53.8 all-gather.2
  100.4 47.3 all-gather.4
  160.7 77.1 reduce-scatter.3
where the time goes:
time: 282 us
  waiting for transfers between devices  197 us (70%)
  blocking collectives  33.3 us (12%)
  matrix products  18.9 us (7%)
  between operations  13.3 us (5%)
  starting transfers between devices  9.73 us (3%)
  local copies, waits for them, and re-layouts  7.46 us (3%)
    unnamed x4, waiting for transfers between devices  78.1 us
    all_gather x1, waiting for transfers between devices, body(): lax.all_gather(out_weight, 'dp', axis=0, tiled=True)  55.3 us
    all_gather x1, waiting for transfers between devices, body(): picked = lax.all_gather(mine, 'dp', axis=0, tiled=True)  44.6 us
    all_to_all x1, blocking collectives, body(): back = lax.all_to_all(added, 'dp', 0, 0, tiled=True)  21.5 us
    all_to_all x1, blocking collectives, body(): mine = lax.all_to_all(slots, 'expert', 0, 3, tiled=True)  11.8 us
    all_to_all x1, waiting for transfers between devices, body(): pieces = lax.all_to_all(split, 'dp', 0, 0, tiled=True)  11.3 us
    all_to_all x1, waiting for transfers between devices, body(): outs = lax.all_to_all(summed, 'expert', 0, 0, tiled=True)  7.45 us
    dot_general x1, matrix products, body(): gate = jnp.dot(picked, w_gate, preferred_element_type=jnp.float32)  5.92 us
  transfers between devices with their start and end apart: 5, of which 5 were waited for; matrix products, arithmetic and copies ran while one was open for 1% of the time, Pallas kernels for 0%

commit v1 on v0

--- a/solution.py
+++ b/solution.py
@@ -5,6 +5,10 @@
 
 BLK = 128
 CAP = 4
+_supply_heaps = lambda values: jnp.concatenate(
+    lax.all_to_all(jnp.stack(lax.axis_size("dp") * [values]), "dp", split_axis=0, concat_axis=0),
+    axis=0,
+)
 
 
 def body(
@@ -40,7 +44,7 @@
     slots = slots.reshape(n_expert, CAP, piece, local_width)
     mine = lax.all_to_all(slots, "expert", 0, 3, tiled=True)
     mine = mine.reshape(CAP * piece, model_width)
-    picked = lax.all_gather(mine, "dp", axis=0, tiled=True)
+    picked = _supply_heaps(mine)
     w_gate = gate_weight[0]
     w_up = up_weight[0]
     w_down = down_weight[0]

time: 282 us -> 309 us (1.096)
  waiting for transfers between devices: 197 us -> 214 us
  starting transfers between devices: 9.73 us -> 14.4 us
    all_to_all x0 -> x1, waiting for transfers between devices: none -> 59.7 us  [lax.all_to_all(jnp.stack(lax.axis_size('dp') * [values]), 'dp', split_axi...]
    all_gather x1 -> x0, waiting for transfers between devices: 44.6 us -> none  [body(): picked = lax.all_gather(mine, 'dp', axis=0, tiled=True)]
    all_to_all x0 -> x1, starting transfers between devices: none -> 4.68 us  [lax.all_to_all(jnp.stack(lax.axis_size('dp') * [values]), 'dp', split_axi...]
    unnamed x4 -> x3, waiting for transfers between devices: 78.1 us -> 80.7 us
where the time goes in v1:
time: 309 us; the launch traced here: 308 us
  waiting for transfers between devices  214 us (69%)
  blocking collectives  33.2 us (11%)
  matrix products  21.2 us (7%)
  starting transfers between devices  14.4 us (5%)
  between operations  13.6 us (4%)
  local copies, waits for them, and re-layouts  9.09 us (3%)
    unnamed x3, waiting for transfers between devices  80.7 us
    all_to_all x1, waiting for transfers between devices, lax.all_to_all(jnp.stack(lax.axis_size('dp') * [values]), 'dp', split_axi...  59.7 us
    all_gather x1, waiting for transfers between devices, body(): lax.all_gather(out_weight, 'dp', axis=0, tiled=True)  55.3 us
    all_to_all x1, blocking collectives, body(): back = lax.all_to_all(added, 'dp', 0, 0, tiled=True)  21.5 us
    all_to_all x1, blocking collectives, body(): mine = lax.all_to_all(slots, 'expert', 0, 3, tiled=True)  11.8 us
    all_to_all x1, waiting for transfers between devices, body(): pieces = lax.all_to_all(split, 'dp', 0, 0, tiled=True)  11.4 us
    all_to_all x1, waiting for transfers between devices, body(): outs = lax.all_to_all(summed, 'expert', 0, 0, tiled=True)  7.45 us
  transfers between devices with their start and end apart: 5, of which 5 were waited for; matrix products, arithmetic and copies ran while one was open for 1% of the time, Pallas kernels for 0%

profile of v1, /device:TPU:0, one launch (start us, length us, event | category | flops | bytes accessed | tf_op | source)
XLA Modules:
  0.0 308.4 jit_solution(16790370662543826187)
XLA Ops:
  6.5 0.0 all-gather.2.cloned.1.call-start
  6.5 0.7 all-gather.2.cloned.1.call-update
  7.3 0.8 copy.29
  8.0 0.1 reshape.97
  8.1 0.0 copy-start
  8.1 55.3 %all-gather.2.cloned.1.call-done = bf16[4096,512]{1,0:T(8,128)(2,1)} async-done(((bf16[256,512]{1,0:T(8,128)(2,1)}), bf16[4096,512]{1,0:T(8,128)(2,1)}) %all-gather.2.cloned.1.call-update) | async-done | bytes 4194320 | tf_op jit(solution)/shard_map/all_gather | solution.py:36
  63.4 5.9 %fusion.8 = bf16[512,512]{1,0:T(8,128)(2,1)S(1)} fusion(bf16[512,4096]{1,0:T(8,128)(2,1)} %param.9, bf16[4096,512]{1,0:T(8,128)(2,1)} %all-gather.2.cloned.1.call-done, bf16[512,512]{1,0:T(8,128)(2,1)} %param.11), kind=kOutput, calls=%fused_computation.9 | convolution fusion | flops 2148270080 | bytes 9437184 | tf_op jit(solution)/shard_map/dot_general | solution.py:34
  69.3 0.8 copy.49
  70.1 5.3 %all-to-all-start = ((bf16[16,4,8,512]{3,2,1,0:T(8,128)(2,1)}), bf16[16,4,8,512]{3,2,1,0:T(8,128)(2,1)S(1)}, u32[]{:S(2)}, u32[]{:S(2)}) async-start(bf16[16,4,8,512]{3,2,1,0:T(8,128)(2,1)} %bitcast.61), calls=%async_computation | async-start | bytes 1048576 | tf_op jit(solution)/shard_map/all_to_all | solution.py:41
  75.4 0.0 copy-done
  75.4 0.1 copy.30
  75.5 11.4 %all-to-all-done = bf16[16,4,8,512]{3,2,1,0:T(8,128)(2,1)S(1)} async-done(((bf16[16,4,8,512]{3,2,1,0:T(8,128)(2,1)}), bf16[16,4,8,512]{3,2,1,0:T(8,128)(2,1)S(1)}, u32[]{:S(2)}, u32[]{:S(2)}) %all-to-all-start) | async-done | bytes 524320 | tf_op jit(solution)/shard_map/all_to_all | solution.py:41
  86.9 0.6 gather_fusion
  87.4 0.1 broadcast_select_fusion
  87.5 11.8 %all_to_all.35 = bf16[8,4,8,512]{3,2,1,0:T(8,128)(2,1)S(1)} all-to-all(bf16[8,4,8,512]{3,2,1,0:T(8,128)(2,1)S(1)} %broadcast_select_fusion), channel_id=1, replica_groups=mesh['dp'=16,'expert'=8] {'expert'}, dimensions={0} | all-to-all | bytes 524288 | tf_op jit(solution)/shard_map/all_to_all | solution.py:45
  99.3 0.1 copy.50
  99.5 0.1 copy.41
  99.6 2.5 stack.3
  102.0 0.0 copy-start.1
  102.0 0.0 copy-start.4
  102.0 4.7 %all-to-all-start.2 = ((bf16[16,32,4096]{2,1,0:T(8,128)(2,1)}), bf16[16,32,4096]{2,1,0:T(8,128)(2,1)}, u32[]{:S(2)}, u32[]{:S(2)}) async-start(bf16[16,32,4096]{2,1,0:T(8,128)(2,1)} %stack.3), calls=%async_computation.2 | async-start | bytes 8388608 | tf_op jit(solution)/shard_map/all_to_all | solution.py:9
  106.7 0.0 reduce-scatter.4.cloned.1.call-start
  106.8 0.5 broadcast.97
  107.3 0.0 copy-done.1
  107.3 0.7 reduce.3
  108.0 0.1 squeeze.20
  108.1 0.0 copy-done.4
  108.1 0.6 dynamic_slice.4
  108.7 0.7 select_bitcast_fusion
  109.4 0.1 mul.19
  109.5 59.7 %all-to-all-done.2 = bf16[16,32,4096]{2,1,0:T(8,128)(2,1)} async-done(((bf16[16,32,4096]{2,1,0:T(8,128)(2,1)}), bf16[16,32,4096]{2,1,0:T(8,128)(2,1)}, u32[]{:S(2)}, u32[]{:S(2)}) %all-to-all-start.2) | async-done | bytes 4194336 | tf_op jit(solution)/shard_map/all_to_all | solution.py:9
  169.1 0.0 copy-start.2
  169.1 5.9 %fusion.3 = f32[512,512]{1,0:T(8,128)S(1)} fusion(bf16[512,4096]{1,0:T(8,128)(2,1)} %bitcast.9, bf16[1,4096,512]{2,1,0:T(8,128)(2,1)} %param.12), kind=kOutput, calls=%fused_computation.5 | convolution fusion | flops 2147483648 | bytes 9437184 | tf_op jit(solution)/shard_map/dot_general | solution.py:56
  175.1 0.0 copy-done.2
  175.1 0.0 copy-start.3
  175.1 4.8 %fusion.9 = bf16[512,512]{1,0:T(8,128)(2,1)S(1)} fusion(bf16[512,4096]{1,0:T(8,128)(2,1)} %bitcast.9, bf16[1,4096,512]{2,1,0:T(8,128)(2,1)S(1)} %copy-done.2, f32[512,512]{1,0:T(8,128)S(1)} %fusion.3), kind=kOutput, calls=%fused_computation.10 | convolution fusion | flops 2149056512 | bytes 9961472 | tf_op jit(solution)/shard_map/dot_general | solution.py:57
  179.9 0.0 copy-done.3
  179.9 4.3 %multiply_convert_fusion = bf16[512,4096]{1,0:T(8,128)(2,1)} fusion(bf16[512,512]{1,0:T(8,128)(2,1)S(1)} %fusion.9, bf16[1,512,4096]{2,1,0:T(8,128)(2,1)S(1)} %copy-done.3, f32[512]{0:T(512)S(1)} %mul.19), kind=kOutput, calls=%fused_computation.1 | convolution fusion | flops 2151677952 | bytes 8914944 | tf_op jit(solution)/shard_map/dot_general | solution.py:59
  184.2 0.0 reduce-scatter.4.cloned.1.call-update
  184.2 79.9 %reduce-scatter.4.cloned.1.call-done = bf16[1,32,4096]{2,1,0:T(8,128)(2,1)} async-done(((bf16[16,32,4096]{2,1,0:T(8,128)(2,1)}), bf16[1,32,4096]{2,1,0:T(8,128)(2,1)}) %reduce-scatter.4.cloned.1.call-update) | async-done | bytes 262160
  264.1 1.0 copy.42
  265.2 0.8 copy.35
  266.0 4.4 %all-to-all-start.3 = ((bf16[8,32,512]{2,1,0:T(8,128)(2,1)}), bf16[8,32,512]{2,1,0:T(8,128)(2,1)S(1)}, u32[]{:S(2)}, u32[]{:S(2)}) async-start(bf16[8,32,512]{2,1,0:T(8,128)(2,1)} %copy.35), calls=%async_computation.3 | async-start | bytes 524288 | tf_op jit(solution)/shard_map/all_to_all | solution.py:65
  270.4 0.1 eq.26
  270.5 7.5 %all-to-all-done.3 = bf16[8,32,512]{2,1,0:T(8,128)(2,1)S(1)} async-done(((bf16[8,32,512]{2,1,0:T(8,128)(2,1)}), bf16[8,32,512]{2,1,0:T(8,128)(2,1)S(1)}, u32[]{:S(2)}, u32[]{:S(2)}) %all-to-all-start.3) | async-done | bytes 262176 | tf_op jit(solution)/shard_map/all_to_all | solution.py:65
  277.9 0.1 reshape.101
  278.1 0.3 fusion.13
  278.4 0.6 copy.37
  279.0 21.5 %all_to_all.36 = f32[16,4,8,512]{3,2,1,0:T(8,128)S(1)} all-to-all(f32[16,4,8,512]{3,2,1,0:T(8,128)S(1)} %copy.37), channel_id=1, replica_groups=mesh['dp'=16,'expert'=8] {'dp'}, dimensions={0} | all-to-all | bytes 2097152 | tf_op jit(solution)/shard_map/all_to_all | solution.py:70
  300.5 0.1 copy.38
  300.6 1.0 fusion.12
  (5 shorter events, 0.0 us)
Async XLA Ops:
  6.5 56.9 %all-gather.2.cloned.1.call-start = ((), (), s32[]{:S(2)}) async-start(), calls=%async_computation.6 | async-start | bytes 4456448 | tf_op jit(solution)/shard_map/all_gather | solution.py:36
  8.1 67.3 %copy-start = (s32[8,4]{0,1:T(4,128)S(1)}, s32[8,4]{0,1:T(4,128)}, u32[]{:S(2)}) copy-start(s32[8,4]{0,1:T(4,128)} %param.16) | copy-start | bytes 388
  70.1 16.8 %all-to-all-start = ((bf16[16,4,8,512]{3,2,1,0:T(8,128)(2,1)}), bf16[16,4,8,512]{3,2,1,0:T(8,128)(2,1)S(1)}, u32[]{:S(2)}, u32[]{:S(2)}) async-start(bf16[16,4,8,512]{3,2,1,0:T(8,128)(2,1)} %bitcast.61), calls=%async_computation | async-start | bytes 1048576 | tf_op jit(solution)/shard_map/all_to_all | solution.py:41
  102.0 5.3 %copy-start.1 = (f32[1,512]{1,0:T(1,128)S(1)}, f32[1,512]{1,0:T(1,128)}, u32[]{:S(2)}) copy-start(f32[1,512]{1,0:T(1,128)} %param.15) | copy-start | bytes 6148
  102.0 6.0 %copy-start.4 = (s32[8]{0:T(128)S(1)}, s32[8]{0:T(128)}, u32[]{:S(2)}) copy-start(s32[8]{0:T(128)} %param.17) | copy-start | bytes 100
  102.0 67.1 %all-to-all-start.2 = ((bf16[16,32,4096]{2,1,0:T(8,128)(2,1)}), bf16[16,32,4096]{2,1,0:T(8,128)(2,1)}, u32[]{:S(2)}, u32[]{:S(2)}) async-start(bf16[16,32,4096]{2,1,0:T(8,128)(2,1)} %stack.3), calls=%async_computation.2 | async-start | bytes 8388608 | tf_op jit(solution)/shard_map/all_to_all | solution.py:9
  106.7 157.4 %reduce-scatter.4.cloned.1.call-start = ((), (), s32[]{:S(2)}) async-start(), calls=%async_computation.7 | async-start | bytes 4456448
  169.1 5.9 %copy-start.2 = (bf16[1,4096,512]{2,1,0:T(8,128)(2,1)S(1)}, bf16[1,4096,512]{2,1,0:T(8,128)(2,1)}, u32[]{:S(2)}) copy-start(bf16[1,4096,512]{2,1,0:T(8,128)(2,1)} %param.13) | copy-start | bytes 12582916
  175.1 4.8 %copy-start.3 = (bf16[1,512,4096]{2,1,0:T(8,128)(2,1)S(1)}, bf16[1,512,4096]{2,1,0:T(8,128)(2,1)}, u32[]{:S(2)}) copy-start(bf16[1,512,4096]{2,1,0:T(8,128)(2,1)} %param.14) | copy-start | bytes 12582916
  266.0 12.0 %all-to-all-start.3 = ((bf16[8,32,512]{2,1,0:T(8,128)(2,1)}), bf16[8,32,512]{2,1,0:T(8,128)(2,1)S(1)}, u32[]{:S(2)}, u32[]{:S(2)}) async-start(bf16[8,32,512]{2,1,0:T(8,128)(2,1)} %copy.35), calls=%async_computation.3 | async-start | bytes 524288 | tf_op jit(solution)/shard_map/all_to_all | solution.py:65
Sparse Core Ops, SparseCore 0:
  9.5 53.8 all-gather.1
  184.3 79.7 reduce-scatter.3
